TPU v7x, 32 devices: a whole 2x2x4 slice. The times are simulated.
32 devices in a mesh: row: 4 (over z), col: 2 (over x), rep: 4 (over y, core).
Axes of the slice: x: 2, y: 2, z: 4, core: 2. Of those that a mesh axis runs over, the one named last changes fastest.
Arguments:
- density: bfloat16 [1536, 1536], P('row', 'col'), as said below
- keep_square: int32 [12, 12], P('row', 'col'), may hold values 0 or 1
- keep_cube: int32 [12, 12], P('row', 'col'), may hold values 0 or 1
Outputs:
- purified: float32 [1536, 1536], P(('row', 'rep'), 'col')
Inputs may be any that keep to these rules, and one draw needn't show every extreme that they name: density is symmetric; its 128 x 128 diagonal blocks are always occupied, any other block may be zero or occupied at any distance from the diagonal.
All inputs are finite; a program needn't handle non-finite values. No bound on the sum of `keep_square` or of `keep_cube` on one device may be relied on, other than what follows from the above.
Results may differ from a plain program's by a relative error of at most 0.002.
Values may be sent and summed in bfloat16 or wider, within the bound.
A program may use at most 64 MiB of HBM per device.

v0:
```python
import jax
import jax.numpy as jnp
from jax import lax
from jax.sharding import PartitionSpec as P

BLK = 128


def broadcast(array, axis, root):
    mine = lax.axis_index(axis) == root
    return lax.psum(jnp.where(mine, array, jnp.zeros_like(array)), axis)


def widen(mask, tile_rows, tile_cols):
    blocks = jnp.broadcast_to(
        mask.astype(jnp.float32)[:, None, :, None], (mask.shape[0], BLK, mask.shape[1], BLK)
    )
    return blocks.reshape(tile_rows, tile_cols)


def left_piece(tile, piece_index):
    height = tile.shape[0]
    per_tile = tile.shape[1] // height
    column = lax.dynamic_slice_in_dim(tile, piece_index % per_tile * height, height, 1)
    return broadcast(column, "col", piece_index // per_tile)


def right_piece(density, piece_index):
    return broadcast(density, "row", piece_index)


def local(density, keep_square, keep_cube):
    tile_rows, tile_cols = density.shape
    rep_count = lax.axis_size("rep")
    row_count = lax.axis_size("row")
    rep_index = lax.axis_index("rep")
    sections = row_count // rep_count
    indices = [position * rep_count + rep_index for position in range(sections)]
    square_total = jnp.zeros((tile_rows, tile_cols), jnp.float32)
    for piece_index in indices:
        right_panel = right_piece(density, piece_index)
        square_total = square_total + jnp.dot(
            left_piece(density, piece_index), right_panel, preferred_element_type=jnp.float32
        )
    square_total = square_total * widen(keep_square, tile_rows, tile_cols)
    square_own = lax.psum_scatter(square_total, "rep", scatter_dimension=0, tiled=True)
    square_low = lax.all_gather(square_own.astype(jnp.bfloat16), "rep", axis=0, tiled=True)
    cube_total = jnp.zeros((tile_rows, tile_cols), jnp.float32)
    for number, piece_index in enumerate(indices):
        right_panel = right_piece(density, piece_index)
        cube_total = cube_total + jnp.dot(
            left_piece(square_low, piece_index), right_panel, preferred_element_type=jnp.float32
        )
    cube_total = cube_total * widen(keep_cube, tile_rows, tile_cols)
    cube_own = lax.psum_scatter(cube_total, "rep", scatter_dimension=0, tiled=True)
    return 3.0 * square_own - 2.0 * cube_own


def solution(mesh):
    return jax.shard_map(
        local,
        mesh=mesh,
        in_specs=(P("row", "col"), P("row", "col"), P("row", "col")),
        out_specs=P(("row", "rep"), "col"),
        check_vma=False,
    )
```

profile of v0, /device:TPU:0, one launch (start us, length us, event | category | flops | bytes accessed | tf_op | source)
XLA Modules:
  0.0 175.6 jit_solution(14447856597460182150)
XLA Ops:
  6.5 0.0 all-reduce.4.cloned.1.call-start
  6.5 1.8 %dynamic-slice_select_fusion.1 = bf16[384,384]{1,0:T(8,128)(2,1)} fusion(bf16[384,768]{1,0:T(8,128)(2,1)} %param.3, s32[]{:T(128)S(6)} %select_n.43, pred[]{:T(512)S(6)} %eq.11), kind=kLoop, calls=%fused_computation.5 | loop fusion | flops 147456 | bytes 589829 | tf_op jit(solution)/shard_map/jit(_where)/select_n | solution.py:11
  8.3 0.0 all-reduce.4.cloned.1.call-update
  8.4 0.0 all-reduce.6.cloned.1.call-start
  8.4 0.0 copy-done.1
  8.4 0.9 broadcast_select_fusion
  9.3 0.0 all-reduce.6.cloned.1.call-update
  9.3 0.0 reduce-scatter.3.cloned.1.call-start
  9.4 0.0 copy-done.5
  9.4 26.7 %all-reduce.4.cloned.1.call-done = bf16[384,384]{1,0:T(8,128)(2,1)} async-done(((bf16[384,384]{1,0:T(8,128)(2,1)}), bf16[384,384]{1,0:T(8,128)(2,1)}) %all-reduce.4.cloned.1.call-update) | async-done | bytes 294928 | tf_op jit(solution)/shard_map/psum | solution.py:11
  36.1 42.0 %all-reduce.6.cloned.1.call-done = bf16[384,768]{1,0:T(8,128)(2,1)} async-done(((bf16[384,768]{1,0:T(8,128)(2,1)}), bf16[384,768]{1,0:T(8,128)(2,1)}) %all-reduce.6.cloned.1.call-update) | async-done | bytes 589840 | tf_op jit(solution)/shard_map/psum | solution.py:11
  78.1 0.2 broadcast_in_dim.4
  78.3 0.0 copy-done.3
  78.3 0.9 copy-done
  79.2 1.5 convolution_multiply_fusion.1
  80.7 0.0 reduce-scatter.3.cloned.1.call-update
  80.7 0.0 copy-start.6
  80.7 0.0 all-reduce.8.cloned.1.call-start
  80.8 25.2 %reduce-scatter.3.cloned.1.call-done = f32[96,768]{1,0:T(8,128)} async-done(((f32[384,768]{1,0:T(8,128)}), f32[96,768]{1,0:T(8,128)}) %reduce-scatter.3.cloned.1.call-update) | async-done | bytes 294928 | tf_op jit(solution)/shard_map/reduce_scatter | solution.py:46
  105.9 1.0 convert_element_type.10
  106.9 6.9 %all_gather.3 = bf16[384,768]{1,0:T(8,128)(2,1)S(1)} all-gather(bf16[96,768]{1,0:T(8,128)(2,1)S(1)} %convert_element_type.10), channel_id=1, replica_groups=mesh['row'=4,'col'=2,'rep'=4] {'rep'}, dimensions={0}, use_global_device_ids=true | all-gather | bytes 737280 | tf_op jit(solution)/shard_map/all_gather | solution.py:47
  113.9 0.8 dynamic-slice_select_fusion
  114.6 0.0 all-reduce.8.cloned.1.call-update
  114.7 0.0 reduce-scatter.5.cloned.1.call-start
  114.7 0.0 copy-done.6
  114.7 24.3 %all-reduce.8.cloned.1.call-done = bf16[384,384]{1,0:T(8,128)(2,1)} async-done(((bf16[384,384]{1,0:T(8,128)(2,1)}), bf16[384,384]{1,0:T(8,128)(2,1)}) %all-reduce.8.cloned.1.call-update) | async-done | bytes 294928 | tf_op jit(solution)/shard_map/psum | solution.py:11
  139.1 0.2 broadcast_in_dim.5
  139.2 0.8 copy-done.4
  140.0 1.5 convolution_multiply_fusion
  141.5 0.0 reduce-scatter.5.cloned.1.call-update
  141.5 25.8 %reduce-scatter.5.cloned.1.call-done = f32[96,768]{1,0:T(8,128)} async-done(((f32[384,768]{1,0:T(8,128)}), f32[96,768]{1,0:T(8,128)}) %reduce-scatter.5.cloned.1.call-update) | async-done | bytes 294928 | tf_op jit(solution)/shard_map/reduce_scatter | solution.py:55
  167.3 1.7 multiply_subtract_fusion
  (9 shorter events, 0.0 us)
Async XLA Ops:
  6.5 1.9 %copy-start.1 = (bf16[384,768]{1,0:T(8,128)(2,1)S(1)}, bf16[384,768]{1,0:T(8,128)(2,1)}, u32[]{:S(2)}) copy-start(bf16[384,768]{1,0:T(8,128)(2,1)} %param.3) | copy-start | bytes 1769476
  6.5 29.5 %all-reduce.4.cloned.1.call-start = ((), (), s32[]{:S(2)}) async-start(), calls=%async_computation.2 | async-start | bytes 589824 | tf_op jit(solution)/shard_map/psum | solution.py:11
  8.3 1.0 copy-start.5
  8.4 69.7 %all-reduce.6.cloned.1.call-start = ((), (), s32[]{:S(2)}) async-start(), calls=%async_computation.3 | async-start | bytes 1179648 | tf_op jit(solution)/shard_map/psum | solution.py:11
  9.3 96.6 %reduce-scatter.3.cloned.1.call-start = ((), (), s32[]{:S(2)}) async-start(), calls=%async_computation.4 | async-start | bytes 1474560 | tf_op jit(solution)/shard_map/reduce_scatter | solution.py:46
  36.1 42.2 %copy-start.3 = (bf16[384,384]{1,0:T(8,128)(2,1)S(1)}, bf16[384,384]{1,0:T(8,128)(2,1)}, u32[]{:S(2)}) copy-start(bf16[384,384]{1,0:T(8,128)(2,1)} %all-reduce.4.cloned.1.call-done) | copy-start | bytes 884740
  78.1 1.1 copy-start
  80.7 34.0 %copy-start.6 = (s32[3,6]{1,0:T(4,128)S(1)}, s32[3,6]{1,0:T(4,128)}, u32[]{:S(2)}) copy-start(s32[3,6]{1,0:T(4,128)} %param.5) | copy-start | bytes 220
  80.7 58.4 %all-reduce.8.cloned.1.call-start = ((), (), s32[]{:S(2)}) async-start(), calls=%async_computation.5 | async-start | bytes 589824 | tf_op jit(solution)/shard_map/psum | solution.py:11
  114.7 52.7 %reduce-scatter.5.cloned.1.call-start = ((), (), s32[]{:S(2)}) async-start(), calls=%async_computation.6 | async-start | bytes 1474560 | tf_op jit(solution)/shard_map/reduce_scatter | solution.py:55
  139.1 1.0 copy-start.4
  141.5 25.8 %copy-start.2 = (f32[96,768]{1,0:T(8,128)S(1)}, f32[96,768]{1,0:T(8,128)}, u32[]{:S(2)}) copy-start(f32[96,768]{1,0:T(8,128)} %reduce-scatter.3.cloned.1.call-done) | copy-start | bytes 884740
Sparse Core Ops, SparseCore 0:
  9.6 26.4 all-reduce.3
  38.4 39.6 all-reduce.5
  80.8 25.0 reduce-scatter.2
  114.8 24.2 all-reduce.7
  141.7 25.6 reduce-scatter.4
where the time goes:
time: 176 us
  waiting for transfers between devices  144 us (82%)
  between operations  13.2 us (8%)
  blocking collectives  6.95 us (4%)
  other arithmetic  6.12 us (3%)
  matrix products  3 us (2%)
  local copies, waits for them, and re-layouts  2.03 us (1%)
    psum x3, waiting for transfers between devices, broadcast(): return lax.psum(jnp.where(mine, array, jnp.zeros_like(array)), axis)  93 us
    reduce_scatter x1, waiting for transfers between devices, local(): lax.psum_scatter(cube_total, 'rep', scatter_dimension=0, tiled=True)  25.8 us
    reduce_scatter x1, waiting for transfers between devices, local(): lax.psum_scatter(square_total, 'rep', scatter_dimension=0, tiled=True)  25.2 us
    all_gather x1, blocking collectives, local(): lax.all_gather(square_own.astype(jnp.bfloat16), 'rep', axis=0, tiled=True)  6.95 us
  transfers between devices with their start and end apart: 5, of which 5 were waited for; matrix products, arithmetic and copies ran while one was open for 0% of the time, Pallas kernels for 0%

commit v1 on v0

v1 whole, which is shorter than its diff:
```python
import functools

import jax
import jax.numpy as jnp
from jax import lax
from jax.experimental import pallas as pl
from jax.experimental.pallas import tpu as pltpu
from jax.sharding import PartitionSpec as P

MESH = pl.DeviceIdType.MESH


def flip(index, bit):
    return index + bit - 2 * bit * (index // bit % 2)


def kernel(rows, cols, reps, block, chunks, density, keep_square, keep_cube, out,
           panel, left, low, total, z_send, z_recv, r_send, r_recv, a_send, a_recv,
           l_send, l_recv, local_sem):
    tile_rows, tile_cols = density.shape
    own = tile_rows // reps
    piece = own // chunks
    ratio = tile_cols // tile_rows
    z, c, p = lax.axis_index("row"), lax.axis_index("col"), lax.axis_index("rep")
    bits = []
    bit = reps // 2
    while bit:
        bits.append(bit)
        bit //= 2
    others = [lax.rem(c + step, cols) for step in range(1, cols)]

    barrier = pltpu.get_barrier_semaphore()
    for step, ok in ((1, z < rows - 1), (-1, z > 0)):
        @pl.when(ok)
        def _():
            pl.semaphore_signal(barrier, inc=1, device_id={"row": z + step}, device_id_type=MESH)
    for bit in bits:
        pl.semaphore_signal(barrier, inc=1, device_id={"rep": flip(p, bit)}, device_id_type=MESH)
    for other in others:
        pl.semaphore_signal(barrier, inc=1, device_id={"col": other}, device_id_type=MESH)
    keep_tile = pltpu.make_async_copy(
        density, panel.at[pl.ds(pl.multiple_of(z * tile_rows, tile_rows), tile_rows)], local_sem.at[0])
    keep_tile.start()
    keep_left = [
        pltpu.make_async_copy(
            density.at[pl.ds(pl.multiple_of(p * own, own), own), pl.ds(part * tile_rows, tile_rows)],
            left.at[c * ratio + part], local_sem.at[1 + part])
        for part in range(ratio)
    ]
    for copy in keep_left:
        copy.start()
    below, above = (z + rows - 1) // rows, (2 * rows - 2 - z) // rows
    pl.semaphore_wait(barrier, len(bits) + len(others) + below + above)

    def slot(t, member, q):
        return panel.at[pl.ds(pl.multiple_of(t * tile_rows + member * own + q * piece, piece), piece)]

    def z_copy(t, q, step, first=False):
        source = slot(t, p, q)
        if first:
            source = density.at[pl.ds(pl.multiple_of(p * own + q * piece, piece), piece)]
        return pltpu.make_async_remote_copy(
            source, slot(t, p, q), z_send.at[(step + 1) // 2, t, q], z_recv.at[t, q],
            device_id={"row": z + step}, device_id_type=MESH)

    def r_copies(t, q, stage):
        members = [p]
        for bit in bits[:stage]:
            members = members + [flip(member, bit) for member in members]
        peer = flip(p, bits[stage])
        base = 2 ** stage - 1
        return [
            pltpu.make_async_remote_copy(
                slot(t, member, q), slot(t, member, q), r_send.at[base + i, t, q],
                r_recv.at[base + i, t, q], device_id={"rep": peer}, device_id_type=MESH)
            for i, member in enumerate(members)
        ]

    def r_waits(t, q, stage):
        peer = flip(p, bits[stage])
        members = [peer]
        for bit in bits[:stage]:
            members = members + [flip(member, bit) for member in members]
        base = 2 ** stage - 1
        for i, member in enumerate(members):
            pltpu.make_async_remote_copy(
                slot(t, member, q), slot(t, member, q), r_send.at[base + i, t, q],
                r_recv.at[base + i, t, q], device_id={"rep": peer}, device_id_type=MESH).wait_recv()

    def a_copy(owner, peer, part):
        return pltpu.make_async_remote_copy(
            density.at[pl.ds(pl.multiple_of(p * own, own), own), pl.ds(part * tile_rows, tile_rows)],
            left.at[owner * ratio + part], a_send.at[peer, part], a_recv.at[owner, part],
            device_id={"col": peer}, device_id_type=MESH)

    def l_copy(owner, peer, part):
        return pltpu.make_async_remote_copy(
            low.at[owner * ratio + part], low.at[owner * ratio + part],
            l_send.at[peer, part], l_recv.at[owner, part],
            device_id={"col": peer}, device_id_type=MESH)

    ways = ((1, z < rows - 1), (-1, z > 0))
    for q in range(chunks):
        for step, ok in ways:
            @pl.when(ok)
            def _():
                z_copy(z, q, step, True).start()
    for other in others:
        for part in range(ratio):
            a_copy(c, other, part).start()

    def arrivals(distance):
        return ((1, z - distance, z - distance >= 0, z < rows - 1),
                (-1, z + distance, z + distance < rows, z > 0))

    def take(distance):
        for q in range(chunks):
            for step, t, ok, onward in arrivals(distance):
                @pl.when(ok)
                def _():
                    z_copy(t, q, step).wait_recv()

                    @pl.when(onward)
                    def _():
                        z_copy(t, q, step).start()
                    for copy in r_copies(t, q, 0):
                        copy.start()

    def spread(distance, stage):
        for q in range(chunks):
            for step, t, ok, onward in arrivals(distance):
                @pl.when(ok)
                def _():
                    r_waits(t, q, stage - 1)
                    for copy in r_copies(t, q, stage):
                        copy.start()

    def product(factor, t):
        return jnp.dot(factor[t], panel[pl.ds(pl.multiple_of(t * tile_rows, tile_rows), tile_rows), :],
                       preferred_element_type=jnp.float32)

    def use(distance):
        for step, t, ok, onward in arrivals(distance):
            @pl.when(ok)
            def _():
                for q in range(chunks):
                    r_waits(t, q, len(bits) - 1)
                total[...] += product(left, t)

    keep_tile.wait()
    for copy in keep_left:
        copy.wait()
    started = False
    for distance in range(1, rows + len(bits)):
        if distance < rows:
            take(distance)
        for stage in range(1, len(bits)):
            if 1 <= distance - stage < rows:
                spread(distance - stage, stage)
        if not started:
            for other in others:
                for part in range(ratio):
                    a_copy(other, other, part).wait_recv()
            total[...] = product(left, z)
            started = True
        if 1 <= distance - len(bits) < rows:
            use(distance - len(bits))

    row_block = (p * own + lax.broadcasted_iota(jnp.int32, (own, block), 0)) // block

    def widen(keep, column):
        wide = jnp.zeros((own, block), jnp.float32)
        for i in range(tile_rows // block):
            wide = jnp.where(row_block == i, keep[i, column].astype(jnp.float32), wide)
        return wide

    per_part = tile_rows // block
    for column in range(tile_cols // block):
        span = pl.ds(column * block, block)
        square = total[:, span] * widen(keep_square, column)
        total[:, span] = square
        low[c * ratio + column // per_part, :, pl.ds(column % per_part * block, block)] = square.astype(jnp.bfloat16)
    for other in others:
        for part in range(ratio):
            l_copy(c, other, part).start()
    cube = product(low, c * ratio)
    for part in range(1, ratio):
        cube = cube + product(low, c * ratio + part)
    out[...] = cube
    for other in others:
        for part in range(ratio):
            l_copy(other, other, part).wait_recv()
            out[...] += product(low, other * ratio + part)
    for column in range(tile_cols // block):
        span = pl.ds(column * block, block)
        out[:, span] = 3.0 * total[:, span] - 2.0 * (out[:, span] * widen(keep_cube, column))

    for q in range(chunks):
        for step, ok in ways:
            @pl.when(ok)
            def _():
                z_copy(z, q, step, True).wait_send()
        for distance in range(1, rows):
            for step, t, ok, onward in arrivals(distance):
                @pl.when(ok)
                def _():
                    @pl.when(onward)
                    def _():
                        z_copy(t, q, step).wait_send()
                    for stage in range(len(bits)):
                        for copy in r_copies(t, q, stage):
                            copy.wait_send()
    for other in others:
        for part in range(ratio):
            a_copy(c, other, part).wait_send()
            l_copy(c, other, part).wait_send()


def local(rows, cols, reps, mat, density, keep_square, keep_cube):
    tile_rows, tile_cols = density.shape
    block = tile_rows // keep_square.shape[0]
    own = tile_rows // reps
    ratio = tile_cols // tile_rows
    chunks = 2 if own % 32 == 0 else 1
    dma = pltpu.SemaphoreType.DMA
    return pl.pallas_call(
        functools.partial(kernel, rows, cols, reps, block, chunks),
        out_shape=jax.ShapeDtypeStruct((own, tile_cols), jnp.float32),
        in_specs=[
            pl.BlockSpec(memory_space=pl.ANY),
            pl.BlockSpec(memory_space=pltpu.SMEM),
            pl.BlockSpec(memory_space=pltpu.SMEM),
        ],
        out_specs=pl.BlockSpec(memory_space=pltpu.VMEM),
        scratch_shapes=[
            pltpu.VMEM((mat, tile_cols), jnp.bfloat16),
            pltpu.VMEM((rows, own, tile_rows), jnp.bfloat16),
            pltpu.VMEM((rows, own, tile_rows), jnp.bfloat16),
            pltpu.VMEM((own, tile_cols), jnp.float32),
            dma((2, rows, chunks)),
            dma((rows, chunks)),
            dma((reps - 1, rows, chunks)),
            dma((reps - 1, rows, chunks)),
            dma((cols, ratio)),
            dma((cols, ratio)),
            dma((cols, ratio)),
            dma((cols, ratio)),
            dma((1 + ratio,)),
        ],
        compiler_params=pltpu.CompilerParams(collective_id=0, has_side_effects=True),
    )(density, keep_square, keep_cube)


def solution(mesh):
    rows, cols, reps = (mesh.shape[axis] for axis in ("row", "col", "rep"))

    def body(density, keep_square, keep_cube):
        return local(rows, cols, reps, density.shape[0] * rows, density, keep_square, keep_cube)

    return jax.shard_map(
        body,
        mesh=mesh,
        in_specs=(P("row", "col"), P("row", "col"), P("row", "col")),
        out_specs=P(("row", "rep"), "col"),
        check_vma=False,
    )
```

time: 176 us -> 30.9 us (0.18)
  waiting for transfers between devices: 144 us -> 0 us
  Pallas kernels: 0 us -> 29.1 us
  between operations: 13.2 us -> 0.01 us
  blocking collectives: 6.95 us -> 0 us
  other arithmetic: 6.12 us -> 0 us
  matrix products: 3 us -> 0 us
    psum x3 -> x0, waiting for transfers between devices: 93 us -> none  [broadcast(): return lax.psum(jnp.where(mine, array, jnp.zeros_like(array)), axis)]
    reduce_scatter x2 -> x0, waiting for transfers between devices: 50.9 us -> none  [the longest x1 25.8 us: local(): lax.psum_scatter(cube_total, 'rep', scatter_dimension=0, tiled=True)]
    pallas_call x0 -> x1, Pallas kernels: none -> 29.1 us  [local(): pl.pallas_call(functools.partial(kernel, rows, cols, reps, block, chunks)...]
    all_gather x1 -> x0, blocking collectives: 6.95 us -> none  [local(): lax.all_gather(square_own.astype(jnp.bfloat16), 'rep', axis=0, tiled=True)]
    select_n x3 -> x0, other arithmetic: 3.42 us -> none  [broadcast(): return lax.psum(jnp.where(mine, array, jnp.zeros_like(array)), axis)]
    dot_general x2 -> x0, matrix products: 3 us -> none  [the longest x1 1.5 us: local(): jnp.dot(left_piece(density, piece_index), right_panel, preferred_element_...]
  transfers between devices with their start and end apart: 5 -> 0, of which waited for: 5 -> 0; matrix products, arithmetic and copies ran while one was open for 0% -> 0% of each run, Pallas kernels for 0% -> 0%
where the time goes in v1:
time: 30.9 us; the launch traced here: 30.8 us
  Pallas kernels  29.1 us (94%)
  local copies, waits for them, and re-layouts  1.69 us (5%)
    pallas_call x1, Pallas kernels, local(): pl.pallas_call(functools.partial(kernel, rows, cols, reps, block, chunks)...  29.1 us
    unnamed x1, local copies, waits for them, and re-layouts  1.69 us

profile of v1, /device:TPU:0, one launch (start us, length us, event | category | flops | bytes accessed | tf_op | source)
XLA Modules:
  0.0 30.8 jit_solution(11682939062757397733)
XLA Ops:
  0.0 29.1 %shard_map.37 = f32[96,768]{1,0:T(8,128)} custom-call(bf16[384,768]{1,0:T(8,128)(2,1)} %density.1, s32[3,6]{1,0:T(4,128)} %keep_square.1, s32[3,6]{1,0:T(4,128)} %keep_cube.1), custom_call_target="tpu_custom_call" | custom-call | tf_op jit(solution)/shard_map/pallas_call | solution.py:226
  29.1 1.7 %copy.5 = f32[96,768]{1,0:T(8,128)} copy(f32[96,768]{1,0:T(8,128)} %shard_map.37) | data formatting | bytes 589824

commit v2 on v1

--- a/solution.py
+++ b/solution.py
@@ -221,11 +221,11 @@
     block = tile_rows // keep_square.shape[0]
     own = tile_rows // reps
     ratio = tile_cols // tile_rows
-    chunks = 2 if own % 32 == 0 else 1
+    chunks = 3 if own % 48 == 0 else 1
     dma = pltpu.SemaphoreType.DMA
     return pl.pallas_call(
         functools.partial(kernel, rows, cols, reps, block, chunks),
-        out_shape=jax.ShapeDtypeStruct((own, tile_cols), jnp.float32),
+        out_shape=pltpu.VMEM((own, tile_cols), jnp.float32),
         in_specs=[
             pl.BlockSpec(memory_space=pl.ANY),
             pl.BlockSpec(memory_space=pltpu.SMEM),

time: 30.9 us -> 28.9 us (0.935)
  Pallas kernels: 29.1 us -> 28 us
  local copies, waits for them, and re-layouts: 1.69 us -> 0.72 us
    pallas_call x1, Pallas kernels: 29.1 us -> 28 us  [local(): pl.pallas_call(functools.partial(kernel, rows, cols, reps, block, chunks)...]
    unnamed x1, local copies, waits for them, and re-layouts: 1.69 us -> 0.72 us
where the time goes in v2:
time: 28.9 us; the launch traced here: 28.7 us
  Pallas kernels  28 us (97%)
  local copies, waits for them, and re-layouts  0.72 us (2%)
    pallas_call x1, Pallas kernels, local(): pl.pallas_call(functools.partial(kernel, rows, cols, reps, block, chunks)...  28 us
    unnamed x1, local copies, waits for them, and re-layouts  0.72 us

profile of v2, /device:TPU:0, one launch (start us, length us, event | category | flops | bytes accessed | tf_op | source)
XLA Modules:
  0.0 28.7 jit_solution(18210087400019124315)
XLA Ops:
  0.0 28.0 %shard_map.37 = f32[96,768]{1,0:T(8,128)S(1)} custom-call(bf16[384,768]{1,0:T(8,128)(2,1)} %density.1, s32[3,6]{1,0:T(4,128)} %keep_square.1, s32[3,6]{1,0:T(4,128)} %keep_cube.1), custom_call_target="tpu_custom_call" | custom-call | tf_op jit(solution)/shard_map/pallas_call | solution.py:226
  28.0 0.7 %copy.5 = f32[96,768]{1,0:T(8,128)} copy(f32[96,768]{1,0:T(8,128)S(1)} %shard_map.37) | data formatting | bytes 589824

commit v3 on v2

--- a/solution.py
+++ b/solution.py
@@ -216,6 +216,277 @@
             l_copy(c, other, part).wait_send()
 
 
+def mirror(table, rows, cols):
+    last = rows - 1
+    return {(last - z, cols - 1 - c): [(last - i, last - j) for i, j in blocks]
+            for (z, c), blocks in table.items()}
+
+
+def folded_plan():
+    down = {(3, 0): [(3, 1), (3, 0)], (3, 1): [(3, 3)],
+            (2, 0): [(2, 1), (3, 1)], (2, 1): [(2, 2), (2, 3), (3, 3)],
+            (1, 0): [(1, 1), (2, 1), (3, 1)], (1, 1): [(2, 2), (2, 3), (3, 3)]}
+    across = {(0, 1): [(0, 2), (0, 3)], (0, 0): [(2, 1), (3, 1)], (1, 1): [(0, 2), (0, 3)]}
+    rows, cols = 4, 2
+    up = mirror(down, rows, cols)
+    across = {**across, **mirror(across, rows, cols)}
+    ready = {(z, c, z, j): 0.0 for z in range(rows) for c in range(cols) for j in (2 * c, 2 * c + 1)}
+    links = [((z, c), (z - 1, c), down.get((z, c), [])) for z in range(rows - 1, 0, -1) for c in range(cols)]
+    links += [((z, c), (z + 1, c), up.get((z, c), [])) for z in range(rows - 1) for c in range(cols)]
+    links += [((z, c), (z, 1 - c), across.get((z, c), [])) for z in range(rows) for c in range(cols)]
+    received = {(z, c): [] for z in range(rows) for c in range(cols)}
+    for source, target, blocks in links:
+        free = 0.0
+        for block in blocks:
+            free = max(free, ready[source + block]) + 1.0
+            ready[target + block] = free + 0.7
+            received[target].append((free, block))
+    plans = {}
+    for z in range(rows):
+        for c in range(cols):
+            order = [block for _, block in sorted(received[z, c])]
+            plans[z, c] = (down.get((z, c), []), up.get((z, c), []), across.get((z, c), []), order)
+    return plans
+
+
+def folded_kernel(rows, cols, reps, block, chunks, density, keep_square, keep_cube, out,
+                  full, left, low, total, send, arrive, r_send, r_recv, a_send, a_recv,
+                  l_send, l_recv, local_sem):
+    tile_rows, tile_cols = density.shape
+    own = tile_rows // reps
+    piece = own // chunks
+    ratio = tile_cols // tile_rows
+    z, c, p = lax.axis_index("row"), lax.axis_index("col"), lax.axis_index("rep")
+    near, far = reps // 2, 1
+    other = 1 - c
+    plans = folded_plan()
+
+    barrier = pltpu.get_barrier_semaphore()
+    for step, ok in ((1, z < rows - 1), (-1, z > 0)):
+        @pl.when(ok)
+        def _():
+            pl.semaphore_signal(barrier, inc=1, device_id={"row": z + step}, device_id_type=MESH)
+    for bit in (near, far):
+        pl.semaphore_signal(barrier, inc=1, device_id={"rep": flip(p, bit)}, device_id_type=MESH)
+    pl.semaphore_signal(barrier, inc=1, device_id={"col": other}, device_id_type=MESH)
+    keep_tile = [
+        pltpu.make_async_copy(density.at[:, pl.ds(part * tile_rows, tile_rows)],
+                              full.at[z, c * ratio + part], local_sem.at[part])
+        for part in range(ratio)
+    ]
+    own_rows = pl.ds(pl.multiple_of(p * own, own), own)
+    keep_left = [
+        pltpu.make_async_copy(density.at[own_rows, pl.ds(part * tile_rows, tile_rows)],
+                              left.at[c * ratio + part], local_sem.at[ratio + part])
+        for part in range(ratio)
+    ]
+    for copy in keep_tile + keep_left:
+        copy.start()
+    below, above = (z + rows - 1) // rows, (2 * rows - 2 - z) // rows
+    pl.semaphore_wait(barrier, 3 + below + above)
+
+    def span(member, q):
+        return pl.ds(pl.multiple_of(member * own + q * piece, piece), piece)
+
+    ways = ({"row": z - 1}, {"row": z + 1}, {"col": other})
+
+    def hop(way, b, q, mine=None, wide=False):
+        member = flip(p, near) if wide else p
+        target = full.at[b[0], b[1], span(member, q)]
+        source = target
+        if mine is not None:
+            source = density.at[span(member, q), pl.ds(mine * tile_rows, tile_rows)]
+        return pltpu.make_async_remote_copy(
+            source, target, send.at[3 if wide else way, b[0], b[1], q],
+            (r_recv.at[0, b[0], b[1], q] if wide else arrive.at[b[0], b[1], q]),
+            device_id=ways[way], device_id_type=MESH)
+
+    def near_copy(b, q, member):
+        ref = full.at[b[0], b[1], span(member, q)]
+        return pltpu.make_async_remote_copy(
+            ref, ref, r_send.at[0, b[0], b[1], q], r_recv.at[0, b[0], b[1], q],
+            device_id={"rep": flip(p, near)}, device_id_type=MESH)
+
+    def far_copy(b, q, which, member):
+        ref = full.at[b[0], b[1], span(member, q)]
+        return pltpu.make_async_remote_copy(
+            ref, ref, r_send.at[which, b[0], b[1], q], r_recv.at[which, b[0], b[1], q],
+            device_id={"rep": flip(p, far)}, device_id_type=MESH)
+
+    def a_copy(owner, part):
+        return pltpu.make_async_remote_copy(
+            density.at[own_rows, pl.ds(part * tile_rows, tile_rows)],
+            left.at[owner * ratio + part], a_send.at[part], a_recv.at[part],
+            device_id={"col": other}, device_id_type=MESH)
+
+    def l_copy(owner, part):
+        return pltpu.make_async_remote_copy(
+            low.at[owner * ratio + part], low.at[owner * ratio + part],
+            l_send.at[part], l_recv.at[part], device_id={"col": other}, device_id_type=MESH)
+
+    class Chip:
+        def __init__(self, row, col):
+            self.row, self.col = row, col
+            self.lists = plans[row, col][:3]
+            self.order = plans[row, col][3]
+            self.mine = [(row, col * ratio + part) for part in range(ratio)]
+            self.theirs = [(row, (1 - col) * ratio + part) for part in range(ratio)]
+            self.have = set(self.mine) | set(self.order)
+            self.wide_out = [b for b in self.lists[2] if b in self.mine]
+            self.wide_in = [b for b in plans[row, 1 - col][2] if b[0] == row and b in self.theirs]
+            self.panel_in = len(self.wide_in) == ratio
+            self.panel_out = len(self.wide_out) == ratio
+
+        def left(self, k):
+            if self.panel_in and (self.row, k) in self.wide_in:
+                return full[self.row, k, own_rows, :]
+            return left[k]
+
+        def product(self, factor, k, part):
+            j = self.col * ratio + part
+            if (k, j) in self.have:
+                return jnp.dot(factor, full[k, j], preferred_element_type=jnp.float32)
+            return lax.dot_general(factor, full[j, k], (((1,), (1,)), ((), ())),
+                                   preferred_element_type=jnp.float32)
+
+        def products_of(self, b):
+            pairs = []
+            if b[1] // ratio == self.col:
+                pairs.append((b[0], b[1] % ratio))
+            if b[0] // ratio == self.col and (b[1], b[0]) not in self.have:
+                pairs.append((b[1], b[0] % ratio))
+            return pairs
+
+        def gather(self):
+            for q in range(chunks):
+                for n in range(3):
+                    for way in range(3):
+                        if n < len(self.lists[way]) and self.lists[way][n] in self.mine:
+                            b = self.lists[way][n]
+                            hop(way, b, q, b[1] % ratio).start()
+                            if way == 2:
+                                hop(way, b, q, b[1] % ratio, True).start()
+            if not self.panel_out:
+                for part in range(ratio):
+                    a_copy(self.col, part).start()
+            items = [(b, q) for b in self.order for q in range(chunks)]
+            lag = 2
+            ready = {b[1] for b in self.mine}
+            waiting, seen = [], set()
+
+            def flush():
+                for k, part in list(waiting):
+                    if k in ready:
+                        where = pl.ds(part * tile_rows, tile_rows)
+                        value = self.product(self.left(k), k, part)
+                        if part in seen:
+                            total[:, where] += value
+                        else:
+                            total[:, where] = value
+                            seen.add(part)
+                        waiting.remove((k, part))
+
+            for n in range(len(items) + 2 * lag):
+                if n < len(items):
+                    b, q = items[n]
+                    hop(0, b, q).wait_recv()
+                    for way in range(3):
+                        if b in self.lists[way]:
+                            hop(way, b, q).start()
+                    if b not in self.wide_in:
+                        near_copy(b, q, p).start()
+                    far_copy(b, q, 1, p).start()
+                    if self.panel_in and b in self.wide_in and q == chunks - 1:
+                        ready.add(b[1])
+                if 0 <= n - lag < len(items):
+                    b, q = items[n - lag]
+                    near_copy(b, q, flip(p, near)).wait_recv()
+                    far_copy(b, q, 2, flip(p, near)).start()
+                if n == 2 * lag:
+                    for copy in keep_tile + keep_left:
+                        copy.wait()
+                    if not self.panel_in:
+                        for part in range(ratio):
+                            a_copy(1 - self.col, part).wait_recv()
+                            ready.add((1 - self.col) * ratio + part)
+                    for b in self.mine:
+                        waiting += self.products_of(b)
+                    flush()
+                if 0 <= n - 2 * lag < len(items):
+                    b, q = items[n - 2 * lag]
+                    far_copy(b, q, 1, flip(p, far)).wait_recv()
+                    far_copy(b, q, 2, flip(flip(p, near), far)).wait_recv()
+                    if q == chunks - 1:
+                        waiting += self.products_of(b)
+                        flush()
+
+        def cube(self):
+            for part in range(ratio):
+                where = pl.ds(part * tile_rows, tile_rows)
+                value = self.product(low[self.mine[0][1]], self.mine[0][1], part)
+                for b in self.mine[1:]:
+                    value = value + self.product(low[b[1]], b[1], part)
+                out[:, where] = value
+            for number, b in enumerate(self.theirs):
+                l_copy(1 - self.col, number).wait_recv()
+                for part in range(ratio):
+                    where = pl.ds(part * tile_rows, tile_rows)
+                    out[:, where] += self.product(low[b[1]], b[1], part)
+
+        def drain(self):
+            for q in range(chunks):
+                for way in range(3):
+                    for b in self.lists[way]:
+                        hop(way, b, q).wait_send()
+                        if way == 2 and b in self.mine:
+                            hop(way, b, q, None, True).wait_send()
+                for b in self.order:
+                    if b not in self.wide_in:
+                        near_copy(b, q, p).wait_send()
+                    far_copy(b, q, 1, p).wait_send()
+                    far_copy(b, q, 2, flip(p, near)).wait_send()
+            if not self.panel_out:
+                for part in range(ratio):
+                    a_copy(self.col, part).wait_send()
+
+    def each_chip(action):
+        for row in range(rows):
+            for col in range(cols):
+                @pl.when((z == row) & (c == col))
+                def _():
+                    action(Chip(row, col))
+
+    each_chip(Chip.gather)
+    widen = widener(p, own, block, tile_rows)
+    per_part = tile_rows // block
+    for column in range(tile_cols // block):
+        where = pl.ds(column * block, block)
+        square = total[:, where] * widen(keep_square, column)
+        total[:, where] = square
+        low[c * ratio + column // per_part, :, pl.ds(column % per_part * block, block)] = square.astype(jnp.bfloat16)
+        if column % per_part == per_part - 1:
+            l_copy(c, column // per_part).start()
+    each_chip(Chip.cube)
+    for column in range(tile_cols // block):
+        where = pl.ds(column * block, block)
+        out[:, where] = 3.0 * total[:, where] - 2.0 * (out[:, where] * widen(keep_cube, column))
+    for part in range(ratio):
+        l_copy(c, part).wait_send()
+    each_chip(Chip.drain)
+
+
+def widener(p, own, block, tile_rows):
+    row_block = (p * own + lax.broadcasted_iota(jnp.int32, (own, block), 0)) // block
+
+    def widen(keep, column):
+        wide = jnp.zeros((own, block), jnp.float32)
+        for i in range(tile_rows // block):
+            wide = jnp.where(row_block == i, keep[i, column].astype(jnp.float32), wide)
+        return wide
+
+    return widen
+
+
 def local(rows, cols, reps, mat, density, keep_square, keep_cube):
     tile_rows, tile_cols = density.shape
     block = tile_rows // keep_square.shape[0]
@@ -223,8 +494,26 @@
     ratio = tile_cols // tile_rows
     chunks = 3 if own % 48 == 0 else 1
     dma = pltpu.SemaphoreType.DMA
+    vmem = pltpu.VMEM
+    folded = (rows, cols, ratio, reps) == (4, 2, 2, 4)
+    body = folded_kernel if folded else kernel
+    scratch = [
+        vmem((rows, rows, tile_rows, tile_rows), jnp.bfloat16),
+        vmem((rows, own, tile_rows), jnp.bfloat16),
+        vmem((rows, own, tile_rows), jnp.bfloat16),
+        vmem((own, tile_cols), jnp.float32),
+        dma((4, rows, rows, chunks)),
+        dma((rows, rows, chunks)),
+        dma((reps - 1, rows, rows, chunks)),
+        dma((reps - 1, rows, rows, chunks)),
+        dma((ratio,)),
+        dma((ratio,)),
+        dma((ratio,)),
+        dma((ratio,)),
+        dma((2 * ratio,)),
+    ]
     return pl.pallas_call(
-        functools.partial(kernel, rows, cols, reps, block, chunks),
+        functools.partial(body, rows, cols, reps, block, chunks),
         out_shape=pltpu.VMEM((own, tile_cols), jnp.float32),
         in_specs=[
             pl.BlockSpec(memory_space=pl.ANY),
@@ -232,7 +521,7 @@
             pl.BlockSpec(memory_space=pltpu.SMEM),
         ],
         out_specs=pl.BlockSpec(memory_space=pltpu.VMEM),
-        scratch_shapes=[
+        scratch_shapes=scratch if folded else [
             pltpu.VMEM((mat, tile_cols), jnp.bfloat16),
             pltpu.VMEM((rows, own, tile_rows), jnp.bfloat16),
             pltpu.VMEM((rows, own, tile_rows), jnp.bfloat16),

time: 28.9 us -> 45.3 us (1.57)
  Pallas kernels: 28 us -> 44.4 us
    pallas_call x1, Pallas kernels: 28 us -> 44.4 us  [local(): pl.pallas_call(functools.partial(body, rows, cols, reps, block, chunks),...]
where the time goes in v3:
time: 45.3 us; the launch traced here: 45.1 us
  Pallas kernels  44.4 us (98%)
  local copies, waits for them, and re-layouts  0.72 us (2%)
    pallas_call x1, Pallas kernels, local(): pl.pallas_call(functools.partial(body, rows, cols, reps, block, chunks),...  44.4 us

profile of v3, /device:TPU:0, one launch (start us, length us, event | category | flops | bytes accessed | tf_op | source)
XLA Modules:
  0.0 45.1 jit_solution(4279045416134044327)
XLA Ops:
  0.0 44.4 %shard_map.37 = f32[96,768]{1,0:T(8,128)S(1)} custom-call(bf16[384,768]{1,0:T(8,128)(2,1)} %density.1, s32[3,6]{1,0:T(4,128)} %keep_square.1, s32[3,6]{1,0:T(4,128)} %keep_cube.1), custom_call_target="tpu_custom_call" | custom-call | tf_op jit(solution)/shard_map/pallas_call | solution.py:515
  44.4 0.7 %copy.5 = f32[96,768]{1,0:T(8,128)} copy(f32[96,768]{1,0:T(8,128)S(1)} %shard_map.37) | data formatting | bytes 589824

commit v4 on v2

--- a/solution.py
+++ b/solution.py
@@ -55,12 +55,17 @@
     def slot(t, member, q):
         return panel.at[pl.ds(pl.multiple_of(t * tile_rows + member * own + q * piece, piece), piece)]
 
-    def z_copy(t, q, step, first=False):
+    def packed(t, place):
+        return t - (t - place - 1 + rows) // rows
+
+    def z_copy(t, q, step, first=False, sending=True):
+        at = z if sending else z - step
         source = slot(t, p, q)
         if first:
             source = density.at[pl.ds(pl.multiple_of(p * own + q * piece, piece), piece)]
         return pltpu.make_async_remote_copy(
-            source, slot(t, p, q), z_send.at[(step + 1) // 2, t, q], z_recv.at[t, q],
+            source, slot(t, p, q), z_send.at[t + (1 - step) // 2, q],
+            z_recv.at[packed(t, at + step), q],
             device_id={"row": z + step}, device_id_type=MESH)
 
     def r_copies(t, q, stage):
@@ -71,8 +76,8 @@
         base = 2 ** stage - 1
         return [
             pltpu.make_async_remote_copy(
-                slot(t, member, q), slot(t, member, q), r_send.at[base + i, t, q],
-                r_recv.at[base + i, t, q], device_id={"rep": peer}, device_id_type=MESH)
+                slot(t, member, q), slot(t, member, q), r_send.at[base + i, packed(t, z), q],
+                r_recv.at[base + i, packed(t, z), q], device_id={"rep": peer}, device_id_type=MESH)
             for i, member in enumerate(members)
         ]
 
@@ -84,8 +89,8 @@
         base = 2 ** stage - 1
         for i, member in enumerate(members):
             pltpu.make_async_remote_copy(
-                slot(t, member, q), slot(t, member, q), r_send.at[base + i, t, q],
-                r_recv.at[base + i, t, q], device_id={"rep": peer}, device_id_type=MESH).wait_recv()
+                slot(t, member, q), slot(t, member, q), r_send.at[base + i, packed(t, z), q],
+                r_recv.at[base + i, packed(t, z), q], device_id={"rep": peer}, device_id_type=MESH).wait_recv()
 
     def a_copy(owner, peer, part):
         return pltpu.make_async_remote_copy(
@@ -118,7 +123,7 @@
             for step, t, ok, onward in arrivals(distance):
                 @pl.when(ok)
                 def _():
-                    z_copy(t, q, step).wait_recv()
+                    z_copy(t, q, step, sending=False).wait_recv()
 
                     @pl.when(onward)
                     def _():
@@ -237,10 +242,10 @@
             pltpu.VMEM((rows, own, tile_rows), jnp.bfloat16),
             pltpu.VMEM((rows, own, tile_rows), jnp.bfloat16),
             pltpu.VMEM((own, tile_cols), jnp.float32),
-            dma((2, rows, chunks)),
-            dma((rows, chunks)),
-            dma((reps - 1, rows, chunks)),
-            dma((reps - 1, rows, chunks)),
+            dma((rows + 1, chunks)),
+            dma((rows - 1, chunks)),
+            dma((reps - 1, rows - 1, chunks)),
+            dma((reps - 1, rows - 1, chunks)),
             dma((cols, ratio)),
             dma((cols, ratio)),
             dma((cols, ratio)),

time: 28.9 us -> 28.6 us (0.990)
  Pallas kernels: 28 us -> 27.7 us
where the time goes in v4:
time: 28.6 us; the launch traced here: 28.5 us
  Pallas kernels  27.7 us (97%)
  local copies, waits for them, and re-layouts  0.72 us (3%)
    pallas_call x1, Pallas kernels, local(): pl.pallas_call(functools.partial(kernel, rows, cols, reps, block, chunks)...  27.7 us
    unnamed x1, local copies, waits for them, and re-layouts  0.72 us

profile of v4, /device:TPU:0, one launch (start us, length us, event | category | flops | bytes accessed | tf_op | source)
XLA Modules:
  0.0 28.5 jit_solution(8486512285188993866)
XLA Ops:
  0.0 27.7 %shard_map.37 = f32[96,768]{1,0:T(8,128)S(1)} custom-call(bf16[384,768]{1,0:T(8,128)(2,1)} %density.1, s32[3,6]{1,0:T(4,128)} %keep_square.1, s32[3,6]{1,0:T(4,128)} %keep_cube.1), custom_call_target="tpu_custom_call" | custom-call | tf_op jit(solution)/shard_map/pallas_call | solution.py:231
  27.7 0.7 %copy.5 = f32[96,768]{1,0:T(8,128)} copy(f32[96,768]{1,0:T(8,128)S(1)} %shard_map.37) | data formatting | bytes 589824
